TPU v7x, 32 devices: a whole 2x2x4 slice. The times are simulated.
32 devices in a mesh: ha: 4 (over z), wa: 8 (over y, x, core).
Axes of the slice: x: 2, y: 2, z: 4, core: 2. Of those that a mesh axis runs over, the one named last changes fastest.
Arguments:
- tokens: bfloat16 [32, 128, 512], P('ha', 'wa'), may hold values from -6 to 6
- cotangent: bfloat16 [32, 128, 512], P('ha', 'wa'), may hold values from -6 to 6
- state_in: float32 [32, 128, 16], P('ha', 'wa'), may hold values from -0.25 to 0.25
- state_out: float32 [32, 128, 16], P('ha', 'wa'), may hold values from -0.25 to 0.25
- width_decay: float32 [32, 128, 8], P('ha', 'wa'), may hold values from -1.6 to 0
- height_decay: float32 [32, 128, 8], P('ha', 'wa'), may hold values from -1.6 to 0
Outputs:
- tokens_grad: float32 [32, 128, 512], P('ha', 'wa')
- state_in_grad: float32 [32, 128, 16], P('ha', 'wa')
- state_out_grad: float32 [32, 128, 16], P('ha', 'wa')
- width_decay_grad: float32 [32, 128, 8], P('ha', 'wa')
- height_decay_grad: float32 [32, 128, 8], P('ha', 'wa')
All inputs are finite; a program needn't handle non-finite values.
Results may differ from a plain program's by a relative error of at most 0.0003.
Values sent between devices are 32-bit elements; how exact they have to be, the bound alone decides.
A program may use at most 128 MiB of HBM per device.

v0:
```python
import functools

import jax
import jax.numpy as jnp
from jax import lax
from jax.experimental import pallas as pl
from jax.experimental.pallas import tpu as pltpu
from jax.sharding import PartitionSpec as P

MESH = pl.DeviceIdType.MESH
F32 = jnp.float32


def kernel(
    ha,
    wa,
    x_in,
    cot_in,
    bt,
    ct,
    wl,
    hl,
    tok_out,
    in_out,
    so_out,
    wg_out,
    hg_out,
    x,
    cot,
    wr,
    hr,
    pw,
    ph,
    rpw,
    rph,
    eh0,
    rh0,
    oh0,
    ih0,
    eh1,
    rh1,
    oh1,
    ih1,
    ew0,
    rw0,
    ow0,
    iw0,
    ew1,
    rw1,
    ow1,
    iw1,
    states,
    grads,
    part,
    send,
    recv,
):
    rows, cols, channels = x_in.shape
    n = bt.shape[1]
    groups = wl.shape[1]
    gw = channels // groups
    split = ew0.shape[0] // rows
    chunk = channels // split
    per_w = rows * split // wa
    per_h = cols // ha
    me_h = lax.axis_index("ha")
    me_w = lax.axis_index("wa")
    place = {"ha": (me_h, ha, per_h), "wa": (me_w, wa, per_w)}

    barrier = pltpu.get_barrier_semaphore()
    for axis in ("ha", "wa"):
        me, count, per = place[axis]
        for d in range(1, count):
            pl.semaphore_signal(
                barrier, inc=1, device_id={axis: lax.rem(me + d, count)}, device_id_type=MESH
            )

    def copies(axis, k, source, target):
        me, count, per = place[axis]
        made = []
        for d in range(1, count):
            peer = lax.rem(me + d, count)
            made.append(
                pltpu.make_async_remote_copy(
                    src_ref=source(peer, per),
                    dst_ref=target(me, per),
                    send_sem=send.at[k, d],
                    recv_sem=recv.at[k, d],
                    device_id={axis: peer},
                    device_id_type=MESH,
                )
            )
        return made

    started = []

    def scatter(axis, k, ends, got):
        made = copies(
            axis, k, lambda peer, per: ends.at[pl.ds(peer * per, per)], lambda me, per: got.at[me]
        )
        for c in made:
            c.start()
        me, count, per = place[axis]
        got[me] = ends[pl.ds(me * per, per)]
        started.extend(made)
        return made

    def give_back(axis, k, result, first):
        made = copies(
            axis, k, lambda peer, per: result.at[peer], lambda me, per: first.at[pl.ds(me * per, per)]
        )
        for c in made:
            c.start()
        me, count, per = place[axis]
        first[pl.ds(me * per, per)] = result[me]
        started.extend(made)
        return made

    def arrive(made):
        for c in made:
            c.wait_recv()

    def put(buffer, i, value):
        for q in range(split):
            buffer[i * split + q] = value[:, q * chunk : (q + 1) * chunk]

    def take(buffer, i):
        return jnp.concatenate([buffer[i * split + q] for q in range(split)], axis=1)

    def chain(axis, got, product, result, backward):
        me, count, per = place[axis]
        order = range(count - 1, -1, -1) if backward else range(count)
        for p in range(per):
            current = jnp.zeros(got.shape[2:], F32)
            for s in order:
                result[s, p] = current
                current = product[s, p] * current + got[s, p]

    def onehot(shape, group_dim):
        g = lax.broadcasted_iota(jnp.int32, shape, group_dim) * gw
        c = lax.broadcasted_iota(jnp.int32, shape, 1 - group_dim)
        return jnp.where((c >= g) & (c < g + gw), 1.0, 0.0).astype(F32)

    def dot(a, b):
        return jnp.dot(a, b, precision=lax.Precision.HIGHEST, preferred_element_type=F32)

    spread = onehot((groups, channels), 0)
    hr[...] = dot(jnp.exp(hl[...]), spread).reshape(rows, cols, channels)
    wr[...] = dot(jnp.exp(wl[...]), spread).reshape(rows, cols, channels)
    x[...] = x_in[...].astype(F32)
    cot[...] = cot_in[...].astype(F32)
    whole = hr[0]
    for i in range(1, rows):
        whole = whole * hr[i]
    for j in range(cols):
        ph[j] = whole[j : j + 1]
    for i in range(rows):
        one = wr[i, 0:1, :]
        for j in range(1, cols):
            one = one * wr[i, j : j + 1, :]
        put(pw, i, one)

    eh0[...] = jnp.zeros_like(eh0)
    eh1[...] = jnp.zeros_like(eh1)

    def col_ends(t, unused):
        i = rows - 1 - t
        columns = ct[i]
        for j in range(cols):
            total = columns[:, j : j + 1] * cot[i, j : j + 1, :] + eh0[j]
            eh0[j] = hr[i, j : j + 1, :] * total
        return unused

    lax.fori_loop(0, rows, col_ends, 0)

    pl.semaphore_wait(barrier, ha + wa - 2)
    got_ph = scatter("ha", 8, ph, rph)
    out_h0 = scatter("ha", 0, eh0, rh0)

    def row_ends(i, unused):
        columns = bt[i]
        carry = columns[:, 0:1] * x[i, 0:1, :]
        for j in range(1, cols):
            carry = wr[i, j : j + 1, :] * carry + columns[:, j : j + 1] * x[i, j : j + 1, :]
        put(ew0, i, carry)
        return unused

    lax.fori_loop(0, rows, row_ends, 0)
    got_pw = scatter("wa", 9, pw, rpw)
    out_w0 = scatter("wa", 1, ew0, rw0)

    arrive(got_ph)
    arrive(out_h0)
    chain("ha", rh0, rph, oh0, True)
    back_h0 = give_back("ha", 4, oh0, ih0)
    arrive(got_pw)
    arrive(out_w0)
    chain("wa", rw0, rpw, ow0, False)
    back_w0 = give_back("wa", 5, ow0, iw0)

    arrive(back_h0)

    def backward(t, unused):
        i = rows - 1 - t
        columns = ct[i]
        carry = jnp.zeros((n, channels), F32)
        for j in range(cols - 1, -1, -1):
            grad = columns[:, j : j + 1] * cot[i, j : j + 1, :] + ih0[j]
            grads[i, j] = grad
            ih0[j] = hr[i, j : j + 1, :] * grad
            carry = wr[i, j : j + 1, :] * (grad + carry)
        put(ew1, i, carry)
        return unused

    lax.fori_loop(0, rows, backward, 0)
    out_w1 = scatter("wa", 2, ew1, rw1)

    arrive(back_w0)

    def forward(i, unused):
        columns = bt[i]
        carry = take(iw0, i)
        for j in range(cols):
            carry = wr[i, j : j + 1, :] * carry + columns[:, j : j + 1] * x[i, j : j + 1, :]
            states[i, j] = carry
            eh1[j] = hr[i, j : j + 1, :] * eh1[j] + carry
        return unused

    lax.fori_loop(0, rows, forward, 0)
    out_h1 = scatter("ha", 3, eh1, rh1)

    arrive(out_w1)
    chain("wa", rw1, rpw, ow1, True)
    back_w1 = give_back("wa", 6, ow1, iw1)
    arrive(out_h1)
    chain("ha", rh1, rph, oh1, False)
    back_h1 = give_back("ha", 7, oh1, ih1)

    lane = lax.broadcasted_iota(jnp.int32, (n, cols), 1)
    arrive(back_w1)

    def rows_done(i, unused):
        columns = bt[i]
        carry = take(iw1, i)
        sums = jnp.zeros((n, cols), F32)
        for j in range(cols - 1, -1, -1):
            grad = grads[i, j] + carry
            carry = wr[i, j : j + 1, :] * grad
            earlier = states[i, j - 1] if j else take(iw0, i)
            part[i, j : j + 1, :] = jnp.sum(grad * earlier, axis=0, keepdims=True)
            tok_out[i, j : j + 1, :] = jnp.sum(grad * columns[:, j : j + 1], axis=0, keepdims=True)
            sums = jnp.where(
                lane == j, jnp.sum(grad * x[i, j : j + 1, :], axis=1, keepdims=True), sums
            )
        in_out[i] = sums
        return unused

    lax.fori_loop(0, rows, rows_done, 0)
    gather = onehot((channels, groups), 1)
    wg_out[...] = jnp.exp(wl[...]) * dot(part[...].reshape(rows * cols, channels), gather)

    arrive(back_h1)

    def cols_done(i, unused):
        sums = jnp.zeros((n, cols), F32)
        for j in range(cols):
            earlier = ih1[j]
            part[i, j : j + 1, :] = jnp.sum(grads[i, j] * earlier, axis=0, keepdims=True)
            total = hr[i, j : j + 1, :] * earlier + states[i, j]
            ih1[j] = total
            sums = jnp.where(
                lane == j, jnp.sum(total * cot[i, j : j + 1, :], axis=1, keepdims=True), sums
            )
        so_out[i] = sums
        return unused

    lax.fori_loop(0, rows, cols_done, 0)
    hg_out[...] = jnp.exp(hl[...]) * dot(part[...].reshape(rows * cols, channels), gather)
    for c in started:
        c.wait_send()


def per_device(ha, wa, tokens, cotangent, state_in, state_out, width_decay, height_decay):
    rows, cols, channels = tokens.shape
    n = state_in.shape[2]
    groups = width_decay.shape[2]
    split = 1 if rows % wa == 0 else wa // rows
    chunk = channels // split
    per_w = rows * split // wa
    per_h = cols // ha
    vmem = pl.BlockSpec(memory_space=pltpu.VMEM)

    def room(*shape):
        return pltpu.VMEM(shape, F32)

    height = [
        room(cols, n, channels),
        room(ha, per_h, n, channels),
        room(ha, per_h, n, channels),
        room(cols, n, channels),
    ]
    width = [
        room(rows * split, n, chunk),
        room(wa, per_w, n, chunk),
        room(wa, per_w, n, chunk),
        room(rows * split, n, chunk),
    ]
    most = max(ha, wa)
    result = pl.pallas_call(
        functools.partial(kernel, ha, wa),
        out_shape=[
            jax.ShapeDtypeStruct((rows, cols, channels), F32),
            jax.ShapeDtypeStruct((rows, n, cols), F32),
            jax.ShapeDtypeStruct((rows, n, cols), F32),
            jax.ShapeDtypeStruct((rows * cols, groups), F32),
            jax.ShapeDtypeStruct((rows * cols, groups), F32),
        ],
        in_specs=[vmem] * 6,
        out_specs=[vmem] * 5,
        scratch_shapes=[room(rows, cols, channels) for _ in range(4)]
        + [
            room(rows * split, 1, chunk),
            room(cols, 1, channels),
            room(wa, per_w, 1, chunk),
            room(ha, per_h, 1, channels),
        ]
        + height
        + height
        + width
        + width
        + [
            room(rows, cols, n, channels),
            room(rows, cols, n, channels),
            room(rows, cols, channels),
            pltpu.SemaphoreType.DMA((10, most)),
            pltpu.SemaphoreType.DMA((10, most)),
        ],
        compiler_params=pltpu.CompilerParams(
            collective_id=0, has_side_effects=True, vmem_limit_bytes=48 * 1024 * 1024
        ),
        name="scan_back",
    )(
        tokens,
        cotangent,
        jnp.swapaxes(state_in, 1, 2),
        jnp.swapaxes(state_out, 1, 2),
        width_decay.reshape(rows * cols, groups),
        height_decay.reshape(rows * cols, groups),
    )
    return (
        result[0],
        jnp.swapaxes(result[1], 1, 2),
        jnp.swapaxes(result[2], 1, 2),
        result[3].reshape(rows, cols, groups),
        result[4].reshape(rows, cols, groups),
    )


def solution(mesh):
    spec = P("ha", "wa", None)
    return jax.shard_map(
        functools.partial(per_device, mesh.shape["ha"], mesh.shape["wa"]),
        mesh=mesh,
        in_specs=(spec,) * 6,
        out_specs=(spec,) * 5,
        check_vma=False,
    )
```

profile of v0, /device:TPU:0, one launch (start us, length us, event | category | flops | bytes accessed | tf_op | source)
XLA Modules:
  0.0 66.8 jit_solution(15597023426450989769)
XLA Ops:
  0.6 0.0 copy-start.2
  0.6 0.0 copy-start.3
  0.7 0.9 %copy.11 = f32[8,16,16]{1,2,0:T(8,128)S(1)} copy(f32[8,16,16]{2,1,0:T(8,128)} %param.8) | data formatting | bytes 16384 | tf_op args[2]
  1.6 0.0 copy-done.2
  1.6 0.0 copy-start.4
  1.6 0.0 copy-start.1
  1.6 0.1 copy.12
  1.7 0.0 copy-start
  1.7 0.0 copy-done.3
  1.7 0.1 copy.13
  1.8 0.6 copy-done.4
  2.4 0.1 copy.14
  2.4 0.1 copy-done.1
  2.5 0.1 copy-done
  2.6 60.6 %scan_back.1 = (f32[8,16,512]{2,1,0:T(8,128)S(1)}, f32[8,16,16]{2,1,0:T(8,128)S(1)}, f32[8,16,16]{2,1,0:T(8,128)S(1)}, f32[128,8]{1,0:T(8,128)S(1)}, f32[128,8]{1,0:T(8,128)S(1)}) custom-call(bf16[8,16,512]{2,1,0:T(8,128)(2,1)S(1)} %copy-done, bf16[8,16,512]{2,1,0:T(8,128)(2,1)S(1)} %copy-done.1, f32[8,16,16]{2,1,0:T(8,128)S(1)} %bitcast.8, ...), custom_call_target="tpu_custom_call" | custom-call | tf_op jit(solution)/shard_map/scan_back/pallas_call | solution.py:309
  63.2 0.7 %copy.15 = f32[8,16,16]{2,1,0:T(8,128)} copy(f32[8,16,16]{1,2,0:T(8,128)S(1)} %bitcast.15) | data formatting | bytes 16384
  63.9 0.7 %copy.17 = f32[8,16,8]{1,2,0:T(8,128)} copy(f32[8,16,8]{2,1,0:T(8,128)S(1)} %bitcast.13) | data formatting | bytes 8192
  64.6 0.7 %copy.18 = f32[8,16,8]{1,2,0:T(8,128)} copy(f32[8,16,8]{2,1,0:T(8,128)S(1)} %bitcast.12) | data formatting | bytes 8192
  65.3 0.7 %copy.16 = f32[8,16,16]{2,1,0:T(8,128)} copy(f32[8,16,16]{1,2,0:T(8,128)S(1)} %bitcast.14) | data formatting | bytes 16384
  66.0 0.7 %copy.20 = f32[8,16,512]{2,1,0:T(8,128)} copy(f32[8,16,512]{2,1,0:T(8,128)S(1)} %get-tuple-element.25) | data formatting | bytes 524288
Async XLA Ops:
  0.6 1.0 %copy-start.2 = (f32[8,16,16]{2,1,0:T(8,128)S(1)}, f32[8,16,16]{2,1,0:T(8,128)}, u32[]{:S(2)}) copy-start(f32[8,16,16]{2,1,0:T(8,128)} %param.9) | copy-start | bytes 24580
  0.6 1.1 %copy-start.3 = (f32[8,16,8]{1,2,0:T(8,128)S(1)}, f32[8,16,8]{1,2,0:T(8,128)}, u32[]{:S(2)}) copy-start(f32[8,16,8]{1,2,0:T(8,128)} %param.10) | copy-start | bytes 12292
  1.6 0.8 %copy-start.4 = (f32[8,16,8]{1,2,0:T(8,128)S(1)}, f32[8,16,8]{1,2,0:T(8,128)}, u32[]{:S(2)}) copy-start(f32[8,16,8]{1,2,0:T(8,128)} %param.11) | copy-start | bytes 12292
  1.6 0.9 %copy-start.1 = (bf16[8,16,512]{2,1,0:T(8,128)(2,1)S(1)}, bf16[8,16,512]{2,1,0:T(8,128)(2,1)}, u32[]{:S(2)}) copy-start(bf16[8,16,512]{2,1,0:T(8,128)(2,1)} %cot_in.1) | copy-start | bytes 393220
  1.7 0.9 %copy-start = (bf16[8,16,512]{2,1,0:T(8,128)(2,1)S(1)}, bf16[8,16,512]{2,1,0:T(8,128)(2,1)}, u32[]{:S(2)}) copy-start(bf16[8,16,512]{2,1,0:T(8,128)(2,1)} %x_in.1) | copy-start | bytes 393220
where the time goes:
time: 67.7 us; the launch traced here: 66.8 us
  Pallas kernels  60.6 us (90%)
  local copies, waits for them, and re-layouts  5.47 us (8%)
  between operations  0.7 us (1%)
    pallas_call x1, Pallas kernels, per_device(): pl.pallas_call(functools.partial(kernel, ha, wa), out_shape=[jax.ShapeDty...  60.6 us
    unnamed x19, local copies, waits for them, and re-layouts  5.47 us

commit v1 on v0

--- a/solution.py
+++ b/solution.py
@@ -189,14 +189,28 @@
     got_pw = scatter("wa", 9, pw, rpw)
     out_w0 = scatter("wa", 1, ew0, rw0)
 
+    arrive(got_pw)
+    arrive(out_w0)
+    chain("wa", rw0, rpw, ow0, False)
+    back_w0 = give_back("wa", 5, ow0, iw0)
     arrive(got_ph)
     arrive(out_h0)
     chain("ha", rh0, rph, oh0, True)
     back_h0 = give_back("ha", 4, oh0, ih0)
-    arrive(got_pw)
-    arrive(out_w0)
-    chain("wa", rw0, rpw, ow0, False)
-    back_w0 = give_back("wa", 5, ow0, iw0)
+
+    arrive(back_w0)
+
+    def forward(i, unused):
+        columns = bt[i]
+        carry = take(iw0, i)
+        for j in range(cols):
+            carry = wr[i, j : j + 1, :] * carry + columns[:, j : j + 1] * x[i, j : j + 1, :]
+            states[i, j] = carry
+            eh1[j] = hr[i, j : j + 1, :] * eh1[j] + carry
+        return unused
+
+    lax.fori_loop(0, rows, forward, 0)
+    out_h1 = scatter("ha", 3, eh1, rh1)
 
     arrive(back_h0)
 
@@ -215,26 +229,12 @@
     lax.fori_loop(0, rows, backward, 0)
     out_w1 = scatter("wa", 2, ew1, rw1)
 
-    arrive(back_w0)
-
-    def forward(i, unused):
-        columns = bt[i]
-        carry = take(iw0, i)
-        for j in range(cols):
-            carry = wr[i, j : j + 1, :] * carry + columns[:, j : j + 1] * x[i, j : j + 1, :]
-            states[i, j] = carry
-            eh1[j] = hr[i, j : j + 1, :] * eh1[j] + carry
-        return unused
-
-    lax.fori_loop(0, rows, forward, 0)
-    out_h1 = scatter("ha", 3, eh1, rh1)
-
+    arrive(out_h1)
+    chain("ha", rh1, rph, oh1, False)
+    back_h1 = give_back("ha", 7, oh1, ih1)
     arrive(out_w1)
     chain("wa", rw1, rpw, ow1, True)
     back_w1 = give_back("wa", 6, ow1, iw1)
-    arrive(out_h1)
-    chain("ha", rh1, rph, oh1, False)
-    back_h1 = give_back("ha", 7, oh1, ih1)
 
     lane = lax.broadcasted_iota(jnp.int32, (n, cols), 1)
     arrive(back_w1)

time: 67.7 us -> 61.5 us (0.908); the launches traced: 66.8 us -> 61.3 us
  Pallas kernels: 60.6 us -> 55.1 us
    pallas_call x1, Pallas kernels: 60.6 us -> 55.1 us  [per_device(): pl.pallas_call(functools.partial(kernel, ha, wa), out_shape=[jax.ShapeDty...]
where the time goes in v1:
time: 61.5 us; the launch traced here: 61.3 us
  Pallas kernels  55.1 us (90%)
  local copies, waits for them, and re-layouts  5.47 us (9%)
  between operations  0.7 us (1%)
    pallas_call x1, Pallas kernels, per_device(): pl.pallas_call(functools.partial(kernel, ha, wa), out_shape=[jax.ShapeDty...  55.1 us
    unnamed x19, local copies, waits for them, and re-layouts  5.47 us

profile of v1, /device:TPU:0, one launch (start us, length us, event | category | flops | bytes accessed | tf_op | source)
XLA Modules:
  0.0 61.3 jit_solution(6372299831276518890)
XLA Ops:
  0.6 0.0 copy-start.2
  0.6 0.0 copy-start.3
  0.7 0.9 %copy.11 = f32[8,16,16]{1,2,0:T(8,128)S(1)} copy(f32[8,16,16]{2,1,0:T(8,128)} %param.8) | data formatting | bytes 16384 | tf_op args[2]
  1.6 0.0 copy-done.2
  1.6 0.0 copy-start.4
  1.6 0.0 copy-start.1
  1.6 0.1 copy.12
  1.7 0.0 copy-start
  1.7 0.0 copy-done.3
  1.7 0.1 copy.13
  1.8 0.6 copy-done.4
  2.4 0.1 copy.14
  2.4 0.1 copy-done.1
  2.5 0.1 copy-done
  2.6 55.1 %scan_back.1 = (f32[8,16,512]{2,1,0:T(8,128)S(1)}, f32[8,16,16]{2,1,0:T(8,128)S(1)}, f32[8,16,16]{2,1,0:T(8,128)S(1)}, f32[128,8]{1,0:T(8,128)S(1)}, f32[128,8]{1,0:T(8,128)S(1)}) custom-call(bf16[8,16,512]{2,1,0:T(8,128)(2,1)S(1)} %copy-done, bf16[8,16,512]{2,1,0:T(8,128)(2,1)S(1)} %copy-done.1, f32[8,16,16]{2,1,0:T(8,128)S(1)} %bitcast.8, ...), custom_call_target="tpu_custom_call" | custom-call | tf_op jit(solution)/shard_map/scan_back/pallas_call | solution.py:309
  57.8 0.7 %copy.15 = f32[8,16,16]{2,1,0:T(8,128)} copy(f32[8,16,16]{1,2,0:T(8,128)S(1)} %bitcast.15) | data formatting | bytes 16384
  58.5 0.7 %copy.17 = f32[8,16,8]{1,2,0:T(8,128)} copy(f32[8,16,8]{2,1,0:T(8,128)S(1)} %bitcast.13) | data formatting | bytes 8192
  59.2 0.7 %copy.18 = f32[8,16,8]{1,2,0:T(8,128)} copy(f32[8,16,8]{2,1,0:T(8,128)S(1)} %bitcast.12) | data formatting | bytes 8192
  59.9 0.7 %copy.16 = f32[8,16,16]{2,1,0:T(8,128)} copy(f32[8,16,16]{1,2,0:T(8,128)S(1)} %bitcast.14) | data formatting | bytes 16384
  60.6 0.7 %copy.20 = f32[8,16,512]{2,1,0:T(8,128)} copy(f32[8,16,512]{2,1,0:T(8,128)S(1)} %get-tuple-element.25) | data formatting | bytes 524288
Async XLA Ops:
  0.6 1.0 %copy-start.2 = (f32[8,16,16]{2,1,0:T(8,128)S(1)}, f32[8,16,16]{2,1,0:T(8,128)}, u32[]{:S(2)}) copy-start(f32[8,16,16]{2,1,0:T(8,128)} %param.9) | copy-start | bytes 24580
  0.6 1.1 %copy-start.3 = (f32[8,16,8]{1,2,0:T(8,128)S(1)}, f32[8,16,8]{1,2,0:T(8,128)}, u32[]{:S(2)}) copy-start(f32[8,16,8]{1,2,0:T(8,128)} %param.10) | copy-start | bytes 12292
  1.6 0.8 %copy-start.4 = (f32[8,16,8]{1,2,0:T(8,128)S(1)}, f32[8,16,8]{1,2,0:T(8,128)}, u32[]{:S(2)}) copy-start(f32[8,16,8]{1,2,0:T(8,128)} %param.11) | copy-start | bytes 12292
  1.6 0.9 %copy-start.1 = (bf16[8,16,512]{2,1,0:T(8,128)(2,1)S(1)}, bf16[8,16,512]{2,1,0:T(8,128)(2,1)}, u32[]{:S(2)}) copy-start(bf16[8,16,512]{2,1,0:T(8,128)(2,1)} %cot_in.1) | copy-start | bytes 393220
  1.7 0.9 %copy-start = (bf16[8,16,512]{2,1,0:T(8,128)(2,1)S(1)}, bf16[8,16,512]{2,1,0:T(8,128)(2,1)}, u32[]{:S(2)}) copy-start(bf16[8,16,512]{2,1,0:T(8,128)(2,1)} %x_in.1) | copy-start | bytes 393220
